TPU v7x, 32 devices: a whole 2x2x4 slice. The times are simulated.
32 devices in a mesh: tile: 8 (over y, x, core), frame: 4 (over z).
Axes of the slice: x: 2, y: 2, z: 4, core: 2. Of those that a mesh axis runs over, the one named last changes fastest.
Arguments:
- video: float32 [16, 16, 160, 128], P('frame', 'tile'), may hold values from -6 to 6
- norm_gain: float32 [2, 2, 128], replicated, may hold values from 0.1 to 1.9
- space_weight: float32 [2, 3, 3, 128, 128], replicated, may hold values from -0.1875 to 0.1875
- time_weight: float32 [2, 3, 128, 128], replicated, may hold values from -0.3125 to 0.3125
- down_weight: float32 [3, 3, 128, 256], replicated, may hold values from -0.1875 to 0.1875
- attn_gain: float32 [256], replicated, may hold values from 0.1 to 1.9
- w_query: float32 [256, 256], replicated, may hold values from -4 to 4
- w_key: float32 [256, 256], replicated, may hold values from -4 to 4
- w_value: float32 [256, 256], replicated, may hold values from -0.375 to 0.375
- w_out: float32 [256, 256], replicated, may hold values from -0.375 to 0.375
Outputs:
- encoded: float32 [32, 320, 256], P(('frame', 'tile'))
All inputs are finite; a program needn't handle non-finite values.
Results may differ from a plain program's by a relative error of at most 0.0003.
Values sent between devices are 32-bit elements; how exact they have to be, the bound alone decides.
No kernel may reach another device: no remote copies, remote signals or barrier semaphores. Data moves between devices by JAX's collectives and lax.ppermute only.
A program may use at most 64 MiB of HBM per device.

v0:
```python
import jax
import jax.numpy as jnp
from jax import lax
from jax.sharding import PartitionSpec as P

highest = lax.Precision.HIGHEST


def passed_along(shard, axis, by):
    size = lax.axis_size(axis)
    pairs = [(i, i + by) for i in range(size) if 0 <= i + by < size]
    return lax.ppermute(shard, axis, pairs)


def extended(cells, sides, width):
    for axis, dim in sides:
        count = lax.axis_size(axis)
        ends = count - 1
        head = lax.slice_in_dim(cells, 0, width, axis=dim)
        tail = lax.slice_in_dim(cells, cells.shape[dim] - width, cells.shape[dim], axis=dim)
        cells = jnp.concatenate(
            [
                lax.ppermute(tail, axis, [(i, (i + 1) % count) for i in range(ends)]),
                cells,
                lax.ppermute(head, axis, [((i + 1) % count, i) for i in range(ends)]),
            ],
            axis=dim,
        )
    return cells


def from_partner(shard, axis, apart):
    return lax.ppermute(shard, axis, [(i, i ^ 1 << apart) for i in range(lax.axis_size(axis))])


def norm(values, gain):
    return values * lax.rsqrt(jnp.mean(values * values, -1, keepdims=True) + 1e-06) * gain


def act(values, gain):
    return jax.nn.silu(norm(values, gain))


def conv_rows(inputs, kernel):
    return lax.conv_general_dilated(
        inputs,
        kernel,
        (1, 1),
        ((0, 0), (1, 1)),
        dimension_numbers=("NHWC", "HWIO", "NHWC"),
        precision=highest,
    )


def time_mix(inputs, kernel):
    earlier = passed_along(inputs[-2:], "frame", 1)
    opening = lax.axis_index("frame") == 0
    start = jnp.where(opening, jnp.concatenate([inputs[:1], inputs[:1]], 0), earlier)
    padded = jnp.concatenate([start, inputs], 0)
    count = inputs.shape[0]
    total = jnp.einsum("fhwc,cd->fhwd", padded[0:count], kernel[0], precision=highest)
    total = total + jnp.einsum("fhwc,cd->fhwd", padded[1 : count + 1], kernel[1], precision=highest)
    total = total + jnp.einsum("fhwc,cd->fhwd", padded[2 : count + 2], kernel[2], precision=highest)
    return total


def fold(carry, query, keys, values):
    best, total, accum = carry
    scores = jnp.dot(query, keys.T, precision=highest)
    new_best = jnp.maximum(best, jnp.max(scores, axis=1))
    factor = jnp.exp(best - new_best)
    weights = jnp.exp(scores - new_best[:, None])
    total = total * factor + jnp.sum(weights, axis=1)
    accum = accum * factor[:, None] + jnp.dot(weights, values, precision=highest)
    return (new_best, total, accum)


def local(
    video,
    norm_gain,
    space_weight,
    time_weight,
    down_weight,
    attn_gain,
    w_query,
    w_key,
    w_value,
    w_out,
):
    frames_dev, rows, width, chans = video.shape
    tiles = lax.axis_size("tile")
    state = video
    for block in range(2):
        wide = extended(act(state, norm_gain[block, 0]), (("tile", 1),), 1)
        mixed = conv_rows(wide, space_weight[block])
        state = state + time_mix(act(mixed, norm_gain[block, 1]), time_weight[block])
    upper = passed_along(state[:, -1:], "tile", 1)
    stacked = jnp.concatenate([upper, state], 1)
    lowered = lax.conv_general_dilated(
        stacked,
        down_weight,
        (2, 2),
        ((0, 0), (1, 0)),
        dimension_numbers=("NHWC", "HWIO", "NHWC"),
        precision=highest,
    )
    outer = lowered.shape[-1]
    group = tiles // frames_dev
    pieces = lowered.reshape(frames_dev * group, -1, outer)
    mine = lax.all_to_all(pieces, "tile", split_axis=0, concat_axis=0, tiled=True).reshape(
        -1, outer
    )
    normed = norm(mine, attn_gain)
    query = jnp.dot(normed, w_query, precision=highest) * float(outer) ** (-0.5)
    count = mine.shape[0]
    carry = (
        jnp.full((count,), -jnp.inf, jnp.float32),
        jnp.zeros((count,), jnp.float32),
        jnp.zeros((count, outer), jnp.float32),
    )
    levels = group.bit_length() - 1
    keys = jnp.dot(normed, w_key, precision=highest)
    values = jnp.dot(normed, w_value, precision=highest)
    carry = fold(carry, query, keys, values)
    for level in range(levels):
        got_keys, got_values = from_partner((keys, values), "tile", level)
        carry = fold(carry, query, got_keys, got_values)
        keys = jnp.concatenate([keys, got_keys], 0)
        values = jnp.concatenate([values, got_values], 0)
    best, total, accum = carry
    attended = accum / total[:, None]
    result = mine + jnp.dot(attended, w_out, precision=highest)
    return result[None]


def solution(mesh):
    in_specs = (P("frame", "tile", None, None), P(), P(), P(), P(), P(), P(), P(), P(), P())
    out_specs = P(("frame", "tile"), None, None)
    return jax.shard_map(local, mesh=mesh, in_specs=in_specs, out_specs=out_specs, check_vma=False)
```

profile of v0, /device:TPU:0, one launch (start us, length us, event | category | flops | bytes accessed | tf_op | source)
XLA Modules:
  0.0 101.9 jit_solution(15611979728672710645)
XLA Ops:
  0.0 0.8 slice_bitcast_fusion.2
  0.8 1.4 %multiply_reduce_fusion.3 = f32[4,2,160]{2,1,0:T(2,128)S(1)} fusion(f32[4,2,160,128]{3,2,1,0:T(8,128)} %param.10), kind=kLoop, calls=%fused_computation.49 | loop fusion | flops 326400 | bytes 660480 | tf_op jit(solution)/shard_map/reduce_sum | solution.py:37
  2.3 1.3 %divide_multiply_fusion.3 = f32[4,2,160,128]{3,2,1,0:T(8,128)S(1)} fusion(f32[4,2,160,128]{3,2,1,0:T(8,128)} %param.10, f32[128]{0:T(128)S(1)} %get-tuple-element.14, f32[4,2,160]{2,1,0:T(2,128)S(1)} %add_rsqrt_fusion.3), kind=kLoop, calls=%fused_computation.48 | loop fusion | flops 983040 | bytes 1316352 | tf_op jit(solution)/shard_map/jit(silu)/mul | solution.py:41
  3.7 2.4 %collective-permute-start = (f32[4,1,160,128]{3,2,1,0:T(8,128)S(1)}, f32[4,1,160,128]{3,2,1,0:T(8,128)S(1)}, u32[]{:S(2)}, u32[]{:S(2)}) collective-permute-start(f32[4,1,160,128]{3,2,1,0:T(8,128)S(1)} %get-tuple-element.9), channel_id=1, source_target_pairs={{0,4},{4,8},{8,12},{12,16},{16,20},{20,24},{24,28},{1,5},{5,9},{9,... | collective-permute-start | bytes 983048 | tf_op jit(solution)/shard_map/ppermute | solution.py:23
  6.1 1.3 %collective-permute-start.1 = (f32[4,1,160,128]{3,2,1,0:T(8,128)S(1)}, f32[4,1,160,128]{3,2,1,0:T(8,128)S(1)}, u32[]{:S(2)}, u32[]{:S(2)}) collective-permute-start(f32[4,1,160,128]{3,2,1,0:T(8,128)S(1)} %get-tuple-element.10), channel_id=1, source_target_pairs={{4,0},{8,4},{12,8},{16,12},{20,16},{24,20},{28,24},{5,1},{9,5},{13... | collective-permute-start | bytes 983048 | tf_op jit(solution)/shard_map/ppermute | solution.py:25
  7.4 4.3 %collective-permute-done.1 = f32[4,1,160,128]{3,2,1,0:T(8,128)S(1)} collective-permute-done((f32[4,1,160,128]{3,2,1,0:T(8,128)S(1)}, f32[4,1,160,128]{3,2,1,0:T(8,128)S(1)}, u32[]{:S(2)}, u32[]{:S(2)}) %collective-permute-start.1) | collective-permute-done | bytes 327712 | tf_op jit(solution)/shard_map/ppermute | solution.py:25
  11.7 0.1 maximum_bitcast_fusion
  11.8 0.8 copy.52
  12.7 0.2 pad.clone
  13.0 0.3 select_maximum_fusion.1
  13.3 0.9 copy-done.2
  14.2 5.3 %multiply_reduce_fusion.1 = (f32[2,32,21]{1,2,0:T(8,128)S(1)}, f32[2,32,21,128]{3,1,2,0:T(8,128)S(1)}) fusion(f32[2,3,3,128,128]{4,3,2,1,0:T(8,128)S(1)} %copy-done.2, f32[4,4,8,23,128]{4,1,3,2,0:T(4,128)S(1)} %select_maximum_fusion.1, pred[32,21]{0,1:T(8,128)(4,1)S(1)} %copy-done.10), kind=kOutput, calls=%fused_computation.37 | convolution fusion | flops 2378685184 | bytes 2793728 | tf_op jit(solution)/shard_map/conv_general_dilated | solution.py:45
  19.5 0.1 copy.32
  19.6 0.1 reshape.110
  19.7 0.5 copy.30
  20.3 0.3 divide_multiply_fusion.2
  20.6 3.5 %collective-permute-start.2 = (f32[2,2,160,128]{3,2,1,0:T(8,128)S(1)}, f32[2,2,160,128]{3,2,1,0:T(8,128)S(1)}, u32[]{:S(2)}, u32[]{:S(2)}) collective-permute-start(f32[2,2,160,128]{3,2,1,0:T(8,128)S(1)} %slice.130), channel_id=1, source_target_pairs={{0,1},{1,2},{2,3},{4,5},{5,6},{6,7},{8,9},{9,10},{10,11},{12,13},{... | collective-permute-start | bytes 983048 | tf_op jit(solution)/shard_map/ppermute | solution.py:12
  24.2 0.7 fusion.40
  24.9 3.8 %collective-permute-done.2 = f32[2,2,160,128]{3,2,1,0:T(8,128)S(1)} collective-permute-done((f32[2,2,160,128]{3,2,1,0:T(8,128)S(1)}, f32[2,2,160,128]{3,2,1,0:T(8,128)S(1)}, u32[]{:S(2)}, u32[]{:S(2)}) %collective-permute-start.2) | collective-permute-done | bytes 327712 | tf_op jit(solution)/shard_map/ppermute | solution.py:12
  28.7 0.7 fusion.22
  29.4 0.9 multiply_reduce_fusion.2
  30.3 0.3 divide_multiply_fusion.1
  30.6 7.2 %collective-permute-start.3 = (f32[4,1,160,128]{3,2,1,0:T(8,128)S(1)}, f32[4,1,160,128]{3,2,1,0:T(8,128)S(1)}, u32[]{:S(2)}, u32[]{:S(2)}) collective-permute-start(f32[4,1,160,128]{3,2,1,0:T(8,128)S(1)} %get-tuple-element.7), channel_id=1, source_target_pairs={{0,4},{4,8},{8,12},{12,16},{16,20},{20,24},{24,28},{1,5},{5,9},{9,... | collective-permute-start | bytes 983048 | tf_op jit(solution)/shard_map/ppermute | solution.py:23
  37.8 1.5 %collective-permute-start.4 = (f32[4,1,160,128]{3,2,1,0:T(8,128)S(1)}, f32[4,1,160,128]{3,2,1,0:T(8,128)S(1)}, u32[]{:S(2)}, u32[]{:S(2)}) collective-permute-start(f32[4,1,160,128]{3,2,1,0:T(8,128)S(1)} %get-tuple-element.8), channel_id=1, source_target_pairs={{4,0},{8,4},{12,8},{16,12},{20,16},{24,20},{28,24},{5,1},{9,5},{13... | collective-permute-start | bytes 983048 | tf_op jit(solution)/shard_map/ppermute | solution.py:25
  39.3 4.8 %collective-permute-done.4 = f32[4,1,160,128]{3,2,1,0:T(8,128)S(1)} collective-permute-done((f32[4,1,160,128]{3,2,1,0:T(8,128)S(1)}, f32[4,1,160,128]{3,2,1,0:T(8,128)S(1)}, u32[]{:S(2)}, u32[]{:S(2)}) %collective-permute-start.4) | collective-permute-done | bytes 327712 | tf_op jit(solution)/shard_map/ppermute | solution.py:25
  44.1 0.1 maximum_bitcast_fusion.1
  44.2 0.8 copy.53
  45.1 0.2 pad.2.clone
  45.3 0.3 select_maximum_fusion
  45.7 0.9 copy-done.3
  46.6 5.3 %multiply_reduce_fusion = (f32[2,32,21]{1,2,0:T(8,128)S(1)}, f32[2,32,21,128]{3,1,2,0:T(8,128)S(1)}) fusion(f32[2,3,3,128,128]{4,3,2,1,0:T(8,128)S(1)} %copy-done.3, f32[4,4,8,23,128]{4,1,3,2,0:T(4,128)S(1)} %select_maximum_fusion, pred[32,21]{0,1:T(8,128)(4,1)S(1)} %copy-done.10), kind=kOutput, calls=%fused_computation.36 | convolution fusion | flops 2378685184 | bytes 2793728 | tf_op jit(solution)/shard_map/conv_general_dilated | solution.py:45
  51.9 0.1 copy.38
  52.0 0.1 reshape.119
  52.1 0.5 copy.36
  52.7 0.3 divide_multiply_fusion
  53.0 4.4 %collective-permute-start.5 = (f32[2,2,160,128]{3,2,1,0:T(8,128)S(1)}, f32[2,2,160,128]{3,2,1,0:T(8,128)S(1)}, u32[]{:S(2)}, u32[]{:S(2)}) collective-permute-start(f32[2,2,160,128]{3,2,1,0:T(8,128)S(1)} %slice.137), channel_id=1, source_target_pairs={{0,1},{1,2},{2,3},{4,5},{5,6},{6,7},{8,9},{9,10},{10,11},{12,13},{... | collective-permute-start | bytes 983048 | tf_op jit(solution)/shard_map/ppermute | solution.py:12
  57.5 0.7 fusion.36
  58.1 3.9 %collective-permute-done.5 = f32[2,2,160,128]{3,2,1,0:T(8,128)S(1)} collective-permute-done((f32[2,2,160,128]{3,2,1,0:T(8,128)S(1)}, f32[2,2,160,128]{3,2,1,0:T(8,128)S(1)}, u32[]{:S(2)}, u32[]{:S(2)}) %collective-permute-start.5) | collective-permute-done | bytes 327712 | tf_op jit(solution)/shard_map/ppermute | solution.py:12
  62.0 0.7 fusion.21
  62.7 0.7 fusion.15
  63.4 8.4 %collective-permute-start.6 = (f32[4,1,160,128]{3,2,1,0:T(8,128)S(1)}, f32[4,1,160,128]{3,2,1,0:T(8,128)S(1)}, u32[]{:S(2)}, u32[]{:S(2)}) collective-permute-start(f32[4,1,160,128]{3,2,1,0:T(8,128)S(1)} %slice.138), channel_id=1, source_target_pairs={{0,4},{4,8},{8,12},{12,16},{16,20},{20,24},{24,28},{1,5},{5,9},{9,... | collective-permute-start | bytes 983048 | tf_op jit(solution)/shard_map/ppermute | solution.py:12
  71.8 1.0 collective-permute-done.6
  72.9 0.6 copy.54
  73.5 0.2 pad.4.clone
  73.7 0.3 select_maximum_fusion.2
  74.0 0.3 copy-done.11
  74.4 1.7 %convolution_select_fusion = f32[1,32,11,256]{3,1,2,0:T(8,128)S(1)} fusion(f32[3,3,128,256]{3,2,1,0:T(8,128)S(1)} %copy-done, f32[3,4,8,24,128]{4,1,3,2,0:T(4,128)S(1)} %select_maximum_fusion.2, pred[32,11]{0,1:T(8,128)(4,1)S(1)} %copy-done.11), kind=kOutput, calls=%fused_computation.19 | convolution fusion | flops 1245798400 | bytes 2720096 | tf_op jit(solution)/shard_map/conv_general_dilated | solution.py:99
  76.1 0.4 copy.42
  76.5 0.2 slice.140
  76.8 17.8 %all_to_all.5 = f32[8,40,256]{2,1,0:T(8,128)S(1)} all-to-all(f32[8,40,256]{2,1,0:T(8,128)S(1)} %bitcast.145), channel_id=1, replica_groups=mesh['tile'=8,'frame'=4] {'tile'}, dimensions={0} | all-to-all | bytes 655360 | tf_op jit(solution)/shard_map/all_to_all | solution.py:110
  94.6 0.1 multiply_reduce_fusion.4
  94.8 0.1 rsqrt.48
  94.9 0.1 fusion.33
  95.0 0.4 fusion.59
  95.4 0.4 fusion.58
  95.9 0.1 collective-permute-start.7
  95.9 0.4 convolution_multiply_fusion
  96.4 0.6 collective-permute-start.8
  96.9 0.7 fusion.56
  97.6 0.7 fusion.57
  98.4 0.2 fusion.31
  98.6 1.1 %fusion.17 = f32[320,256]{1,0:T(8,128)S(1)} fusion(f32[320,256]{1,0:T(8,128)S(1)} %fusion.59, f32[320,320]{0,1:T(8,128)S(1)} %get-tuple-element.23, f32[320]{0:T(512)S(1)} %get-tuple-element.22, f32[320]{0:T(512)S(1)} %get-tuple-element.6, f32[320]{0:T(512)S(1)} %get-tuple-element.11), kind=kOutput, calls=%fused_computation.25 | convolution fusion | flops 314839040 | bytes 1068800 | tf_op jit(solution)/shard_map/dot_general | solution.py:74
  99.7 1.1 %fusion.18 = f32[320,256]{1,0:T(8,128)S(1)} fusion(f32[320,256]{1,0:T(8,128)S(1)} %fusion.17, f32[320,256]{1,0:T(8,128)S(1)} %collective-permute-done.8, f32[320,320]{0,1:T(8,128)S(1)} %get-tuple-element.25, f32[320]{0:T(512)S(1)} %max.13, f32[320]{0:T(512)S(1)} %get-tuple-element.5), kind=kOutput, calls=%fused_computation.26 | convolution fusion | flops 314839040 | bytes 1395200 | tf_op jit(solution)/shard_map/dot_general | solution.py:74
  100.8 1.2 %fusion.16 = f32[1,320,256]{2,1,0:T(8,128)} fusion(f32[320,256]{1,0:T(8,128)S(1)} %bitcast.139, f32[320,256]{1,0:T(8,128)S(1)} %fusion.18, f32[256,256]{1,0:T(8,128)S(1)} %copy-done.9), kind=kOutput, calls=%fused_computation.21 | convolution fusion | flops 251740160 | bytes 1245184 | tf_op jit(solution)/shard_map/dot_general | solution.py:132
  (54 shorter events, 0.6 us)
Async XLA Ops:
  0.0 74.0 %copy-start = (f32[3,3,128,256]{3,2,1,0:T(8,128)S(1)}, f32[3,3,128,256]{3,2,1,0:T(8,128)}, u32[]{:S(2)}) copy-start(f32[3,3,128,256]{3,2,1,0:T(8,128)} %param.14) | copy-start | bytes 3538948
  3.7 3.7 %collective-permute-start = (f32[4,1,160,128]{3,2,1,0:T(8,128)S(1)}, f32[4,1,160,128]{3,2,1,0:T(8,128)S(1)}, u32[]{:S(2)}, u32[]{:S(2)}) collective-permute-start(f32[4,1,160,128]{3,2,1,0:T(8,128)S(1)} %get-tuple-element.9), channel_id=1, source_target_pairs={{0,4},{4,8},{8,12},{12,16},{16,20},{20,24},{24,28},{1,5},{5,9},{9,... | collective-permute-start | bytes 983048 | tf_op jit(solution)/shard_map/ppermute | solution.py:23
  6.1 5.6 %collective-permute-start.1 = (f32[4,1,160,128]{3,2,1,0:T(8,128)S(1)}, f32[4,1,160,128]{3,2,1,0:T(8,128)S(1)}, u32[]{:S(2)}, u32[]{:S(2)}) collective-permute-start(f32[4,1,160,128]{3,2,1,0:T(8,128)S(1)} %get-tuple-element.10), channel_id=1, source_target_pairs={{4,0},{8,4},{12,8},{16,12},{20,16},{24,20},{28,24},{5,1},{9,5},{13... | collective-permute-start | bytes 983048 | tf_op jit(solution)/shard_map/ppermute | solution.py:25
  12.9 1.3 %copy-start.2 = (f32[2,3,3,128,128]{4,3,2,1,0:T(8,128)S(1)}, f32[2,3,3,128,128]{4,3,2,1,0:T(8,128)}, u32[]{:S(2)}) copy-start(f32[2,3,3,128,128]{4,3,2,1,0:T(8,128)} %param.12) | copy-start | bytes 3538948
  12.9 1.3 %copy-start.10 = (pred[32,21]{0,1:T(8,128)(4,1)S(1)}, pred[32,21]{0,1:T(8,128)(4,1)}, u32[]{:S(2)}) copy-start(pred[32,21]{0,1:T(8,128)(4,1)} %constant.47) | copy-start | bytes 2020
  20.3 3.8 %copy-start.4 = (f32[2,3,128,128]{3,2,1,0:T(8,128)S(1)}, f32[2,3,128,128]{3,2,1,0:T(8,128)}, u32[]{:S(2)}) copy-start(f32[2,3,128,128]{3,2,1,0:T(8,128)} %param.13) | copy-start | bytes 1179652
  20.6 8.1 %collective-permute-start.2 = (f32[2,2,160,128]{3,2,1,0:T(8,128)S(1)}, f32[2,2,160,128]{3,2,1,0:T(8,128)S(1)}, u32[]{:S(2)}, u32[]{:S(2)}) collective-permute-start(f32[2,2,160,128]{3,2,1,0:T(8,128)S(1)} %slice.130), channel_id=1, source_target_pairs={{0,1},{1,2},{2,3},{4,5},{5,6},{6,7},{8,9},{9,10},{10,11},{12,13},{... | collective-permute-start | bytes 983048 | tf_op jit(solution)/shard_map/ppermute | solution.py:12
  24.8 4.6 %copy-start.1 = (f32[4,2,160,128]{3,2,1,0:T(8,128)S(1)}, f32[4,2,160,128]{3,2,1,0:T(8,128)}, u32[]{:S(2)}) copy-start(f32[4,2,160,128]{3,2,1,0:T(8,128)} %param.10) | copy-start | bytes 1966084
  30.6 8.7 %collective-permute-start.3 = (f32[4,1,160,128]{3,2,1,0:T(8,128)S(1)}, f32[4,1,160,128]{3,2,1,0:T(8,128)S(1)}, u32[]{:S(2)}, u32[]{:S(2)}) collective-permute-start(f32[4,1,160,128]{3,2,1,0:T(8,128)S(1)} %get-tuple-element.7), channel_id=1, source_target_pairs={{0,4},{4,8},{8,12},{12,16},{16,20},{20,24},{24,28},{1,5},{5,9},{9,... | collective-permute-start | bytes 983048 | tf_op jit(solution)/shard_map/ppermute | solution.py:23
  37.8 6.3 %collective-permute-start.4 = (f32[4,1,160,128]{3,2,1,0:T(8,128)S(1)}, f32[4,1,160,128]{3,2,1,0:T(8,128)S(1)}, u32[]{:S(2)}, u32[]{:S(2)}) collective-permute-start(f32[4,1,160,128]{3,2,1,0:T(8,128)S(1)} %get-tuple-element.8), channel_id=1, source_target_pairs={{4,0},{8,4},{12,8},{16,12},{20,16},{24,20},{28,24},{5,1},{9,5},{13... | collective-permute-start | bytes 983048 | tf_op jit(solution)/shard_map/ppermute | solution.py:25
  45.3 1.3 %copy-start.3 = (f32[2,3,3,128,128]{4,3,2,1,0:T(8,128)S(1)}, f32[2,3,3,128,128]{4,3,2,1,0:T(8,128)}, u32[]{:S(2)}) copy-start(f32[2,3,3,128,128]{4,3,2,1,0:T(8,128)} %param.12) | copy-start | bytes 3538948
  52.7 4.7 %copy-start.5 = (f32[2,3,128,128]{3,2,1,0:T(8,128)S(1)}, f32[2,3,128,128]{3,2,1,0:T(8,128)}, u32[]{:S(2)}) copy-start(f32[2,3,128,128]{3,2,1,0:T(8,128)} %param.13) | copy-start | bytes 1179652
  53.0 9.0 %collective-permute-start.5 = (f32[2,2,160,128]{3,2,1,0:T(8,128)S(1)}, f32[2,2,160,128]{3,2,1,0:T(8,128)S(1)}, u32[]{:S(2)}, u32[]{:S(2)}) collective-permute-start(f32[2,2,160,128]{3,2,1,0:T(8,128)S(1)} %slice.137), channel_id=1, source_target_pairs={{0,1},{1,2},{2,3},{4,5},{5,6},{6,7},{8,9},{9,10},{10,11},{12,13},{... | collective-permute-start | bytes 983048 | tf_op jit(solution)/shard_map/ppermute | solution.py:12
  63.4 9.4 %collective-permute-start.6 = (f32[4,1,160,128]{3,2,1,0:T(8,128)S(1)}, f32[4,1,160,128]{3,2,1,0:T(8,128)S(1)}, u32[]{:S(2)}, u32[]{:S(2)}) collective-permute-start(f32[4,1,160,128]{3,2,1,0:T(8,128)S(1)} %slice.138), channel_id=1, source_target_pairs={{0,4},{4,8},{8,12},{12,16},{16,20},{20,24},{24,28},{1,5},{5,9},{9,... | collective-permute-start | bytes 983048 | tf_op jit(solution)/shard_map/ppermute | solution.py:12
  73.7 0.7 copy-start.11
  76.5 18.3 %copy-start.12 = (f32[256]{0:T(256)S(1)}, f32[256]{0:T(256)}, u32[]{:S(2)}) copy-start(f32[256]{0:T(256)} %param.15) | copy-start | bytes 3076
  76.7 18.2 %copy-start.6 = (f32[256,256]{1,0:T(8,128)S(1)}, f32[256,256]{1,0:T(8,128)}, u32[]{:S(2)}) copy-start(f32[256,256]{1,0:T(8,128)} %param.18) | copy-start | bytes 786436
  76.8 18.6 %copy-start.7 = (f32[256,256]{1,0:T(8,128)S(1)}, f32[256,256]{1,0:T(8,128)}, u32[]{:S(2)}) copy-start(f32[256,256]{1,0:T(8,128)} %param.17) | copy-start | bytes 786436
  94.7 1.2 %copy-start.8 = (f32[256,256]{1,0:T(8,128)S(1)}, f32[256,256]{1,0:T(8,128)}, u32[]{:S(2)}) copy-start(f32[256,256]{1,0:T(8,128)} %param.16) | copy-start | bytes 786436
  95.9 1.8 %collective-permute-start.7 = (f32[320,256]{1,0:T(8,128)S(1)}, f32[320,256]{1,0:T(8,128)S(1)}, u32[]{:S(2)}, u32[]{:S(2)}) collective-permute-start(f32[320,256]{1,0:T(8,128)S(1)} %fusion.58), channel_id=1, source_target_pairs={{0,4},{4,0},{8,12},{12,8},{16,20},{20,16},{24,28},{28,24},{1,5},{5... | collective-permute-start | bytes 983048 | tf_op jit(solution)/shard_map/ppermute | solution.py:33
  96.4 3.3 %collective-permute-start.8 = (f32[320,256]{1,0:T(8,128)S(1)}, f32[320,256]{1,0:T(8,128)S(1)}, u32[]{:S(2)}, u32[]{:S(2)}) collective-permute-start(f32[320,256]{1,0:T(8,128)S(1)} %fusion.59), channel_id=1, source_target_pairs={{0,4},{4,0},{8,12},{12,8},{16,20},{20,16},{24,28},{28,24},{1,5},{5... | collective-permute-start | bytes 983048 | tf_op jit(solution)/shard_map/ppermute | solution.py:33
  98.5 2.2 %copy-start.9 = (f32[256,256]{1,0:T(8,128)S(1)}, f32[256,256]{1,0:T(8,128)}, u32[]{:S(2)}) copy-start(f32[256,256]{1,0:T(8,128)} %param.19) | copy-start | bytes 786436
where the time goes:
time: 102 us
  starting transfers between devices  29.3 us (29%)
  matrix products  22.6 us (22%)
  waiting for transfers between devices  17.8 us (17%)
  blocking collectives  17.8 us (17%)
  local copies, waits for them, and re-layouts  8.5 us (8%)
  other arithmetic  5.25 us (5%)
    all_to_all x1, blocking collectives, local(): lax.all_to_all(pieces, 'tile', split_axis=0, concat_axis=0, tiled=True)  17.8 us
    ppermute x3, starting transfers between devices, passed_along(): return lax.ppermute(shard, axis, pairs)  16.3 us
    conv_general_dilated x2, matrix products, conv_rows(): lax.conv_general_dilated(inputs, kernel, (1, 1), ((0, 0), (1, 1)), dimens...  10.6 us
    ppermute x2, starting transfers between devices, extended(): lax.ppermute(tail, axis, [(i, (i + 1) % count) for i in range(ends)])  9.63 us
    ppermute x2, waiting for transfers between devices, extended(): lax.ppermute(head, axis, [((i + 1) % count, i) for i in range(ends)])  9.07 us
    ppermute x3, waiting for transfers between devices, passed_along(): return lax.ppermute(shard, axis, pairs)  8.69 us
    unnamed x30, local copies, waits for them, and re-layouts  4.61 us
    ppermute x2, starting transfers between devices, extended(): lax.ppermute(head, axis, [((i + 1) % count, i) for i in range(ends)])  2.76 us
  transfers between devices with their start and end apart: 9, of which 5 were waited for; matrix products, arithmetic and copies ran while one was open for 4% of the time, Pallas kernels for 0%

commit v1 on v0

--- a/solution.py
+++ b/solution.py
@@ -4,6 +4,18 @@
 from jax.sharding import PartitionSpec as P
 
 highest = lax.Precision.HIGHEST
+
+
+def exchange_directly(x, axis, split, join):
+    ways, here = (lax.axis_size(axis), lax.axis_index(axis))
+    width = x.shape[split] // ways
+    turned = jnp.roll(x, -here * width, axis=split)
+    got = [lax.slice_in_dim(turned, 0, width, axis=split)]
+    for far in range(1, ways):
+        sent = lax.slice_in_dim(turned, far * width, (far + 1) * width, axis=split)
+        got.append(lax.ppermute(sent, axis, [(d, (d + far) % ways) for d in range(ways)]))
+    line = jnp.concatenate(got[::-1], axis=join)
+    return jnp.roll(line, (here + 1) * got[0].shape[join], axis=join)
 
 
 def passed_along(shard, axis, by):
@@ -107,9 +119,7 @@
     outer = lowered.shape[-1]
     group = tiles // frames_dev
     pieces = lowered.reshape(frames_dev * group, -1, outer)
-    mine = lax.all_to_all(pieces, "tile", split_axis=0, concat_axis=0, tiled=True).reshape(
-        -1, outer
-    )
+    mine = exchange_directly(pieces, "tile", 0, 0).reshape(-1, outer)
     normed = norm(mine, attn_gain)
     query = jnp.dot(normed, w_query, precision=highest) * float(outer) ** (-0.5)
     count = mine.shape[0]

time: 102 us -> 103 us (level)
  blocking collectives: 17.8 us -> 0 us
  starting transfers between devices: 29.3 us -> 42.8 us
  waiting for transfers between devices: 17.8 us -> 22 us
    all_to_all x1 -> x0, blocking collectives: 17.8 us -> none  [local(): lax.all_to_all(pieces, 'tile', split_axis=0, concat_axis=0, tiled=True)]
    ppermute x0 -> x7, starting transfers between devices: none -> 13.5 us  [exchange_directly(): lax.ppermute(sent, axis, [(d, (d + far) % ways) for d in range(ways)])]
    ppermute x0 -> x7, waiting for transfers between devices: none -> 4.26 us  [exchange_directly(): lax.ppermute(sent, axis, [(d, (d + far) % ways) for d in range(ways)])]
    unnamed x30 -> x35, local copies, waits for them, and re-layouts: 4.61 us -> 4.63 us
  transfers between devices with their start and end apart: 9 -> 16, of which waited for: 5 -> 8; matrix products, arithmetic and copies ran while one was open for 4% -> 5% of each run, Pallas kernels for 0% -> 0%
where the time goes in v1:
time: 103 us; the launch traced here: 102 us
  starting transfers between devices  42.8 us (42%)
  matrix products  22.6 us (22%)
  waiting for transfers between devices  22 us (21%)
  local copies, waits for them, and re-layouts  8.56 us (8%)
  other arithmetic  5.35 us (5%)
    ppermute x3, starting transfers between devices, passed_along(): return lax.ppermute(shard, axis, pairs)  16.3 us
    ppermute x7, starting transfers between devices, exchange_directly(): lax.ppermute(sent, axis, [(d, (d + far) % ways) for d in range(ways)])  13.5 us
    conv_general_dilated x2, matrix products, conv_rows(): lax.conv_general_dilated(inputs, kernel, (1, 1), ((0, 0), (1, 1)), dimens...  10.6 us
    ppermute x2, starting transfers between devices, extended(): lax.ppermute(tail, axis, [(i, (i + 1) % count) for i in range(ends)])  9.62 us
    ppermute x2, waiting for transfers between devices, extended(): lax.ppermute(head, axis, [((i + 1) % count, i) for i in range(ends)])  9.08 us
    ppermute x3, waiting for transfers between devices, passed_along(): return lax.ppermute(shard, axis, pairs)  8.67 us
    unnamed x35, local copies, waits for them, and re-layouts  4.63 us
    ppermute x7, waiting for transfers between devices, exchange_directly(): lax.ppermute(sent, axis, [(d, (d + far) % ways) for d in range(ways)])  4.26 us
  transfers between devices with their start and end apart: 16, of which 8 were waited for; matrix products, arithmetic and copies ran while one was open for 5% of the time, Pallas kernels for 0%

profile of v1, /device:TPU:0, one launch (start us, length us, event | category | flops | bytes accessed | tf_op | source)
XLA Modules:
  0.0 102.1 jit_solution(9832999053506938471)
XLA Ops:
  0.0 0.8 slice_bitcast_fusion.2
  0.8 1.4 %multiply_reduce_fusion.3 = f32[4,2,160]{2,1,0:T(2,128)S(1)} fusion(f32[4,2,160,128]{3,2,1,0:T(8,128)} %param.12), kind=kLoop, calls=%fused_computation.53 | loop fusion | flops 326400 | bytes 660480 | tf_op jit(solution)/shard_map/reduce_sum | solution.py:49
  2.3 1.3 %divide_multiply_fusion.3 = f32[4,2,160,128]{3,2,1,0:T(8,128)S(1)} fusion(f32[4,2,160,128]{3,2,1,0:T(8,128)} %param.12, f32[128]{0:T(128)S(1)} %get-tuple-element.24, f32[4,2,160]{2,1,0:T(2,128)S(1)} %add_rsqrt_fusion.3), kind=kLoop, calls=%fused_computation.52 | loop fusion | flops 983040 | bytes 1316352 | tf_op jit(solution)/shard_map/jit(silu)/mul | solution.py:53
  3.7 2.4 %collective-permute-start = (f32[4,1,160,128]{3,2,1,0:T(8,128)S(1)}, f32[4,1,160,128]{3,2,1,0:T(8,128)S(1)}, u32[]{:S(2)}, u32[]{:S(2)}) collective-permute-start(f32[4,1,160,128]{3,2,1,0:T(8,128)S(1)} %get-tuple-element.12), channel_id=1, source_target_pairs={{0,4},{4,8},{8,12},{12,16},{16,20},{20,24},{24,28},{1,5},{5,9},{9,... | collective-permute-start | bytes 983048 | tf_op jit(solution)/shard_map/ppermute | solution.py:35
  6.1 1.3 %collective-permute-start.1 = (f32[4,1,160,128]{3,2,1,0:T(8,128)S(1)}, f32[4,1,160,128]{3,2,1,0:T(8,128)S(1)}, u32[]{:S(2)}, u32[]{:S(2)}) collective-permute-start(f32[4,1,160,128]{3,2,1,0:T(8,128)S(1)} %get-tuple-element.13), channel_id=1, source_target_pairs={{4,0},{8,4},{12,8},{16,12},{20,16},{24,20},{28,24},{5,1},{9,5},{13... | collective-permute-start | bytes 983048 | tf_op jit(solution)/shard_map/ppermute | solution.py:37
  7.4 4.3 %collective-permute-done.1 = f32[4,1,160,128]{3,2,1,0:T(8,128)S(1)} collective-permute-done((f32[4,1,160,128]{3,2,1,0:T(8,128)S(1)}, f32[4,1,160,128]{3,2,1,0:T(8,128)S(1)}, u32[]{:S(2)}, u32[]{:S(2)}) %collective-permute-start.1) | collective-permute-done | bytes 327712 | tf_op jit(solution)/shard_map/ppermute | solution.py:37
  11.8 0.8 copy.52
  12.7 0.2 pad.clone
  13.0 0.3 select_maximum_fusion.1
  13.3 0.9 copy-done.2
  14.2 5.3 %multiply_reduce_fusion.1 = (f32[2,32,21]{1,2,0:T(8,128)S(1)}, f32[2,32,21,128]{3,1,2,0:T(8,128)S(1)}) fusion(f32[2,3,3,128,128]{4,3,2,1,0:T(8,128)S(1)} %copy-done.2, f32[4,4,8,23,128]{4,1,3,2,0:T(4,128)S(1)} %select_maximum_fusion.1, pred[32,21]{0,1:T(8,128)(4,1)S(1)} %copy-done.9), kind=kOutput, calls=%fused_computation.37 | convolution fusion | flops 2378685184 | bytes 2793728 | tf_op jit(solution)/shard_map/conv_general_dilated | solution.py:57
  19.5 0.5 copy.30
  20.1 0.1 copy.32
  20.3 0.3 divide_multiply_fusion.2
  20.6 3.5 %collective-permute-start.2 = (f32[2,2,160,128]{3,2,1,0:T(8,128)S(1)}, f32[2,2,160,128]{3,2,1,0:T(8,128)S(1)}, u32[]{:S(2)}, u32[]{:S(2)}) collective-permute-start(f32[2,2,160,128]{3,2,1,0:T(8,128)S(1)} %slice.162), channel_id=1, source_target_pairs={{0,1},{1,2},{2,3},{4,5},{5,6},{6,7},{8,9},{9,10},{10,11},{12,13},{... | collective-permute-start | bytes 983048 | tf_op jit(solution)/shard_map/ppermute | solution.py:24
  24.2 0.7 fusion.42
  24.9 3.8 %collective-permute-done.2 = f32[2,2,160,128]{3,2,1,0:T(8,128)S(1)} collective-permute-done((f32[2,2,160,128]{3,2,1,0:T(8,128)S(1)}, f32[2,2,160,128]{3,2,1,0:T(8,128)S(1)}, u32[]{:S(2)}, u32[]{:S(2)}) %collective-permute-start.2) | collective-permute-done | bytes 327712 | tf_op jit(solution)/shard_map/ppermute | solution.py:24
  28.7 0.7 fusion.22
  29.4 0.9 multiply_reduce_fusion.2
  30.3 0.3 divide_multiply_fusion.1
  30.6 7.2 %collective-permute-start.3 = (f32[4,1,160,128]{3,2,1,0:T(8,128)S(1)}, f32[4,1,160,128]{3,2,1,0:T(8,128)S(1)}, u32[]{:S(2)}, u32[]{:S(2)}) collective-permute-start(f32[4,1,160,128]{3,2,1,0:T(8,128)S(1)} %get-tuple-element.10), channel_id=1, source_target_pairs={{0,4},{4,8},{8,12},{12,16},{16,20},{20,24},{24,28},{1,5},{5,9},{9,... | collective-permute-start | bytes 983048 | tf_op jit(solution)/shard_map/ppermute | solution.py:35
  37.8 1.5 %collective-permute-start.4 = (f32[4,1,160,128]{3,2,1,0:T(8,128)S(1)}, f32[4,1,160,128]{3,2,1,0:T(8,128)S(1)}, u32[]{:S(2)}, u32[]{:S(2)}) collective-permute-start(f32[4,1,160,128]{3,2,1,0:T(8,128)S(1)} %get-tuple-element.11), channel_id=1, source_target_pairs={{4,0},{8,4},{12,8},{16,12},{20,16},{24,20},{28,24},{5,1},{9,5},{13... | collective-permute-start | bytes 983048 | tf_op jit(solution)/shard_map/ppermute | solution.py:37
  39.3 4.8 %collective-permute-done.4 = f32[4,1,160,128]{3,2,1,0:T(8,128)S(1)} collective-permute-done((f32[4,1,160,128]{3,2,1,0:T(8,128)S(1)}, f32[4,1,160,128]{3,2,1,0:T(8,128)S(1)}, u32[]{:S(2)}, u32[]{:S(2)}) %collective-permute-start.4) | collective-permute-done | bytes 327712 | tf_op jit(solution)/shard_map/ppermute | solution.py:37
  44.2 0.8 copy.53
  45.1 0.2 pad.2.clone
  45.3 0.3 select_maximum_fusion
  45.7 0.9 copy-done.3
  46.6 5.3 %multiply_reduce_fusion = (f32[2,32,21]{1,2,0:T(8,128)S(1)}, f32[2,32,21,128]{3,1,2,0:T(8,128)S(1)}) fusion(f32[2,3,3,128,128]{4,3,2,1,0:T(8,128)S(1)} %copy-done.3, f32[4,4,8,23,128]{4,1,3,2,0:T(4,128)S(1)} %select_maximum_fusion, pred[32,21]{0,1:T(8,128)(4,1)S(1)} %copy-done.9), kind=kOutput, calls=%fused_computation.36 | convolution fusion | flops 2378685184 | bytes 2793728 | tf_op jit(solution)/shard_map/conv_general_dilated | solution.py:57
  51.9 0.5 copy.36
  52.7 0.3 divide_multiply_fusion
  53.0 4.4 %collective-permute-start.5 = (f32[2,2,160,128]{3,2,1,0:T(8,128)S(1)}, f32[2,2,160,128]{3,2,1,0:T(8,128)S(1)}, u32[]{:S(2)}, u32[]{:S(2)}) collective-permute-start(f32[2,2,160,128]{3,2,1,0:T(8,128)S(1)} %slice.169), channel_id=1, source_target_pairs={{0,1},{1,2},{2,3},{4,5},{5,6},{6,7},{8,9},{9,10},{10,11},{12,13},{... | collective-permute-start | bytes 983048 | tf_op jit(solution)/shard_map/ppermute | solution.py:24
  57.4 0.7 fusion.38
  58.1 3.9 %collective-permute-done.5 = f32[2,2,160,128]{3,2,1,0:T(8,128)S(1)} collective-permute-done((f32[2,2,160,128]{3,2,1,0:T(8,128)S(1)}, f32[2,2,160,128]{3,2,1,0:T(8,128)S(1)}, u32[]{:S(2)}, u32[]{:S(2)}) %collective-permute-start.5) | collective-permute-done | bytes 327712 | tf_op jit(solution)/shard_map/ppermute | solution.py:24
  62.0 0.7 fusion.21
  62.7 0.7 fusion.15
  63.4 8.4 %collective-permute-start.6 = (f32[4,1,160,128]{3,2,1,0:T(8,128)S(1)}, f32[4,1,160,128]{3,2,1,0:T(8,128)S(1)}, u32[]{:S(2)}, u32[]{:S(2)}) collective-permute-start(f32[4,1,160,128]{3,2,1,0:T(8,128)S(1)} %slice.170), channel_id=1, source_target_pairs={{0,4},{4,8},{8,12},{12,16},{16,20},{20,24},{24,28},{1,5},{5,9},{9,... | collective-permute-start | bytes 983048 | tf_op jit(solution)/shard_map/ppermute | solution.py:24
  71.8 1.0 collective-permute-done.6
  72.9 0.6 copy.54
  73.5 0.2 pad.4.clone
  73.7 0.3 select_maximum_fusion.2
  74.0 0.3 copy-done.10
  74.4 1.7 %convolution_select_fusion = f32[1,32,11,256]{3,1,2,0:T(8,128)S(1)} fusion(f32[3,3,128,256]{3,2,1,0:T(8,128)S(1)} %copy-done, f32[3,4,8,24,128]{4,1,3,2,0:T(4,128)S(1)} %select_maximum_fusion.2, pred[32,11]{0,1:T(8,128)(4,1)S(1)} %copy-done.10), kind=kOutput, calls=%fused_computation.19 | convolution fusion | flops 1245798400 | bytes 2720096 | tf_op jit(solution)/shard_map/conv_general_dilated | solution.py:111
  76.1 0.4 copy.42
  76.5 0.2 slice.172
  77.0 6.2 %collective-permute-start.8 = (f32[1,40,256]{2,1,0:T(8,128)S(1)}, f32[1,40,256]{2,1,0:T(8,128)S(1)}, u32[]{:S(2)}, u32[]{:S(2)}) collective-permute-start(f32[1,40,256]{2,1,0:T(8,128)S(1)} %get-tuple-element.19), channel_id=1, source_target_pairs={{0,24},{4,28},{8,0},{12,4},{16,8},{20,12},{24,16},{28,20},{1,25},{... | collective-permute-start | bytes 122888 | tf_op jit(solution)/shard_map/ppermute | solution.py:16
  83.2 3.9 %collective-permute-start.9 = (f32[1,40,256]{2,1,0:T(8,128)S(1)}, f32[1,40,256]{2,1,0:T(8,128)S(1)}, u32[]{:S(2)}, u32[]{:S(2)}) collective-permute-start(f32[1,40,256]{2,1,0:T(8,128)S(1)} %get-tuple-element.18), channel_id=1, source_target_pairs={{0,20},{4,24},{8,28},{12,0},{16,4},{20,8},{24,12},{28,16},{1,21},{... | collective-permute-start | bytes 122888 | tf_op jit(solution)/shard_map/ppermute | solution.py:16
  87.1 0.2 collective-permute-start.10
  87.3 1.5 %collective-permute-start.11 = (f32[1,40,256]{2,1,0:T(8,128)S(1)}, f32[1,40,256]{2,1,0:T(8,128)S(1)}, u32[]{:S(2)}, u32[]{:S(2)}) collective-permute-start(f32[1,40,256]{2,1,0:T(8,128)S(1)} %get-tuple-element.16), channel_id=1, source_target_pairs={{0,12},{4,16},{8,20},{12,24},{16,28},{20,0},{24,4},{28,8},{1,13},{... | collective-permute-start | bytes 122888 | tf_op jit(solution)/shard_map/ppermute | solution.py:16
  88.8 1.6 %collective-permute-start.12 = (f32[1,40,256]{2,1,0:T(8,128)S(1)}, f32[1,40,256]{2,1,0:T(8,128)S(1)}, u32[]{:S(2)}, u32[]{:S(2)}) collective-permute-start(f32[1,40,256]{2,1,0:T(8,128)S(1)} %get-tuple-element.15), channel_id=1, source_target_pairs={{0,8},{4,12},{8,16},{12,20},{16,24},{20,28},{24,0},{28,4},{1,9},{5... | collective-permute-start | bytes 122888 | tf_op jit(solution)/shard_map/ppermute | solution.py:16
  90.5 1.0 %collective-permute-done.10 = f32[1,40,256]{2,1,0:T(8,128)S(1)} collective-permute-done((f32[1,40,256]{2,1,0:T(8,128)S(1)}, f32[1,40,256]{2,1,0:T(8,128)S(1)}, u32[]{:S(2)}, u32[]{:S(2)}) %collective-permute-start.10) | collective-permute-done | bytes 40992 | tf_op jit(solution)/shard_map/ppermute | solution.py:16
  91.5 2.2 %collective-permute-done.12 = f32[1,40,256]{2,1,0:T(8,128)S(1)} collective-permute-done((f32[1,40,256]{2,1,0:T(8,128)S(1)}, f32[1,40,256]{2,1,0:T(8,128)S(1)}, u32[]{:S(2)}, u32[]{:S(2)}) %collective-permute-start.12) | collective-permute-done | bytes 40992 | tf_op jit(solution)/shard_map/ppermute | solution.py:16
  93.7 1.1 %collective-permute-done.13 = f32[1,40,256]{2,1,0:T(8,128)S(1)} collective-permute-done((f32[1,40,256]{2,1,0:T(8,128)S(1)}, f32[1,40,256]{2,1,0:T(8,128)S(1)}, u32[]{:S(2)}, u32[]{:S(2)}) %collective-permute-start.13) | collective-permute-done | bytes 40992 | tf_op jit(solution)/shard_map/ppermute | solution.py:16
  94.8 0.1 multiply_reduce_fusion.4
  95.0 0.1 fusion.35
  95.2 0.4 fusion.62
  95.7 0.4 convolution_multiply_fusion
  96.1 0.4 fusion.63
  96.6 0.6 collective-permute-start.15
  97.1 0.7 fusion.60
  97.8 0.7 fusion.61
  98.5 0.2 fusion.31
  98.7 1.1 %fusion.17 = f32[320,256]{1,0:T(8,128)S(1)} fusion(f32[320,256]{1,0:T(8,128)S(1)} %fusion.63, f32[320,320]{0,1:T(8,128)S(1)} %get-tuple-element.33, f32[320]{0:T(512)S(1)} %get-tuple-element.32, f32[320]{0:T(512)S(1)} %get-tuple-element.7, f32[320]{0:T(512)S(1)} %get-tuple-element.21), kind=kOutput, calls=%fused_computation.25 | convolution fusion | flops 314839040 | bytes 1068800 | tf_op jit(solution)/shard_map/dot_general | solution.py:86
  99.8 1.1 %fusion.18 = f32[320,256]{1,0:T(8,128)S(1)} fusion(f32[320,256]{1,0:T(8,128)S(1)} %fusion.17, f32[320,256]{1,0:T(8,128)S(1)} %collective-permute-done.15, f32[320,320]{0,1:T(8,128)S(1)} %get-tuple-element.35, f32[320]{0:T(512)S(1)} %max.13, f32[320]{0:T(512)S(1)} %get-tuple-element.6), kind=kOutput, calls=%fused_computation.26 | convolution fusion | flops 314839040 | bytes 1395200 | tf_op jit(solution)/shard_map/dot_general | solution.py:86
  100.9 1.2 %fusion.16 = f32[1,320,256]{2,1,0:T(8,128)} fusion(f32[320,256]{1,0:T(8,128)S(1)} %bitcast.141, f32[320,256]{1,0:T(8,128)S(1)} %fusion.18, f32[256,256]{1,0:T(8,128)S(1)} %copy-done.8), kind=kOutput, calls=%fused_computation.21 | convolution fusion | flops 251740160 | bytes 1245184 | tf_op jit(solution)/shard_map/dot_general | solution.py:142
  (75 shorter events, 1.4 us)
Async XLA Ops:
  0.0 74.0 %copy-start = (f32[3,3,128,256]{3,2,1,0:T(8,128)S(1)}, f32[3,3,128,256]{3,2,1,0:T(8,128)}, u32[]{:S(2)}) copy-start(f32[3,3,128,256]{3,2,1,0:T(8,128)} %param.16) | copy-start | bytes 3538948
  3.7 3.7 %collective-permute-start = (f32[4,1,160,128]{3,2,1,0:T(8,128)S(1)}, f32[4,1,160,128]{3,2,1,0:T(8,128)S(1)}, u32[]{:S(2)}, u32[]{:S(2)}) collective-permute-start(f32[4,1,160,128]{3,2,1,0:T(8,128)S(1)} %get-tuple-element.12), channel_id=1, source_target_pairs={{0,4},{4,8},{8,12},{12,16},{16,20},{20,24},{24,28},{1,5},{5,9},{9,... | collective-permute-start | bytes 983048 | tf_op jit(solution)/shard_map/ppermute | solution.py:35
  6.1 5.6 %collective-permute-start.1 = (f32[4,1,160,128]{3,2,1,0:T(8,128)S(1)}, f32[4,1,160,128]{3,2,1,0:T(8,128)S(1)}, u32[]{:S(2)}, u32[]{:S(2)}) collective-permute-start(f32[4,1,160,128]{3,2,1,0:T(8,128)S(1)} %get-tuple-element.13), channel_id=1, source_target_pairs={{4,0},{8,4},{12,8},{16,12},{20,16},{24,20},{28,24},{5,1},{9,5},{13... | collective-permute-start | bytes 983048 | tf_op jit(solution)/shard_map/ppermute | solution.py:37
  12.9 1.3 %copy-start.2 = (f32[2,3,3,128,128]{4,3,2,1,0:T(8,128)S(1)}, f32[2,3,3,128,128]{4,3,2,1,0:T(8,128)}, u32[]{:S(2)}) copy-start(f32[2,3,3,128,128]{4,3,2,1,0:T(8,128)} %param.14) | copy-start | bytes 3538948
  12.9 1.3 %copy-start.9 = (pred[32,21]{0,1:T(8,128)(4,1)S(1)}, pred[32,21]{0,1:T(8,128)(4,1)}, u32[]{:S(2)}) copy-start(pred[32,21]{0,1:T(8,128)(4,1)} %constant.71) | copy-start | bytes 2020
  20.1 4.1 %copy-start.4 = (f32[2,3,128,128]{3,2,1,0:T(8,128)S(1)}, f32[2,3,128,128]{3,2,1,0:T(8,128)}, u32[]{:S(2)}) copy-start(f32[2,3,128,128]{3,2,1,0:T(8,128)} %param.15) | copy-start | bytes 1179652
  20.6 8.1 %collective-permute-start.2 = (f32[2,2,160,128]{3,2,1,0:T(8,128)S(1)}, f32[2,2,160,128]{3,2,1,0:T(8,128)S(1)}, u32[]{:S(2)}, u32[]{:S(2)}) collective-permute-start(f32[2,2,160,128]{3,2,1,0:T(8,128)S(1)} %slice.162), channel_id=1, source_target_pairs={{0,1},{1,2},{2,3},{4,5},{5,6},{6,7},{8,9},{9,10},{10,11},{12,13},{... | collective-permute-start | bytes 983048 | tf_op jit(solution)/shard_map/ppermute | solution.py:24
  24.8 4.6 %copy-start.1 = (f32[4,2,160,128]{3,2,1,0:T(8,128)S(1)}, f32[4,2,160,128]{3,2,1,0:T(8,128)}, u32[]{:S(2)}) copy-start(f32[4,2,160,128]{3,2,1,0:T(8,128)} %param.12) | copy-start | bytes 1966084
  30.6 8.7 %collective-permute-start.3 = (f32[4,1,160,128]{3,2,1,0:T(8,128)S(1)}, f32[4,1,160,128]{3,2,1,0:T(8,128)S(1)}, u32[]{:S(2)}, u32[]{:S(2)}) collective-permute-start(f32[4,1,160,128]{3,2,1,0:T(8,128)S(1)} %get-tuple-element.10), channel_id=1, source_target_pairs={{0,4},{4,8},{8,12},{12,16},{16,20},{20,24},{24,28},{1,5},{5,9},{9,... | collective-permute-start | bytes 983048 | tf_op jit(solution)/shard_map/ppermute | solution.py:35
  37.8 6.3 %collective-permute-start.4 = (f32[4,1,160,128]{3,2,1,0:T(8,128)S(1)}, f32[4,1,160,128]{3,2,1,0:T(8,128)S(1)}, u32[]{:S(2)}, u32[]{:S(2)}) collective-permute-start(f32[4,1,160,128]{3,2,1,0:T(8,128)S(1)} %get-tuple-element.11), channel_id=1, source_target_pairs={{4,0},{8,4},{12,8},{16,12},{20,16},{24,20},{28,24},{5,1},{9,5},{13... | collective-permute-start | bytes 983048 | tf_op jit(solution)/shard_map/ppermute | solution.py:37
  45.3 1.3 %copy-start.3 = (f32[2,3,3,128,128]{4,3,2,1,0:T(8,128)S(1)}, f32[2,3,3,128,128]{4,3,2,1,0:T(8,128)}, u32[]{:S(2)}) copy-start(f32[2,3,3,128,128]{4,3,2,1,0:T(8,128)} %param.14) | copy-start | bytes 3538948
  53.0 9.0 %collective-permute-start.5 = (f32[2,2,160,128]{3,2,1,0:T(8,128)S(1)}, f32[2,2,160,128]{3,2,1,0:T(8,128)S(1)}, u32[]{:S(2)}, u32[]{:S(2)}) collective-permute-start(f32[2,2,160,128]{3,2,1,0:T(8,128)S(1)} %slice.169), channel_id=1, source_target_pairs={{0,1},{1,2},{2,3},{4,5},{5,6},{6,7},{8,9},{9,10},{10,11},{12,13},{... | collective-permute-start | bytes 983048 | tf_op jit(solution)/shard_map/ppermute | solution.py:24
  63.4 9.4 %collective-permute-start.6 = (f32[4,1,160,128]{3,2,1,0:T(8,128)S(1)}, f32[4,1,160,128]{3,2,1,0:T(8,128)S(1)}, u32[]{:S(2)}, u32[]{:S(2)}) collective-permute-start(f32[4,1,160,128]{3,2,1,0:T(8,128)S(1)} %slice.170), channel_id=1, source_target_pairs={{0,4},{4,8},{8,12},{12,16},{16,20},{20,24},{24,28},{1,5},{5,9},{9,... | collective-permute-start | bytes 983048 | tf_op jit(solution)/shard_map/ppermute | solution.py:24
  73.7 0.7 copy-start.10
  76.8 18.3 %copy-start.11 = (f32[256]{0:T(256)S(1)}, f32[256]{0:T(256)}, u32[]{:S(2)}) copy-start(f32[256]{0:T(256)} %param.17) | copy-start | bytes 3076
  76.8 18.3 %copy-start.5 = (f32[256,256]{1,0:T(8,128)S(1)}, f32[256,256]{1,0:T(8,128)}, u32[]{:S(2)}) copy-start(f32[256,256]{1,0:T(8,128)} %param.19) | copy-start | bytes 786436
  76.9 11.9 %collective-permute-start.7 = (f32[1,40,256]{2,1,0:T(8,128)S(1)}, f32[1,40,256]{2,1,0:T(8,128)S(1)}, u32[]{:S(2)}, u32[]{:S(2)}) collective-permute-start(f32[1,40,256]{2,1,0:T(8,128)S(1)} %get-tuple-element.20), channel_id=1, source_target_pairs={{0,28},{4,0},{8,4},{12,8},{16,12},{20,16},{24,20},{28,24},{1,29},{... | collective-permute-start | bytes 122888 | tf_op jit(solution)/shard_map/ppermute | solution.py:16
  77.0 13.5 %collective-permute-start.8 = (f32[1,40,256]{2,1,0:T(8,128)S(1)}, f32[1,40,256]{2,1,0:T(8,128)S(1)}, u32[]{:S(2)}, u32[]{:S(2)}) collective-permute-start(f32[1,40,256]{2,1,0:T(8,128)S(1)} %get-tuple-element.19), channel_id=1, source_target_pairs={{0,24},{4,28},{8,0},{12,4},{16,8},{20,12},{24,16},{28,20},{1,25},{... | collective-permute-start | bytes 122888 | tf_op jit(solution)/shard_map/ppermute | solution.py:16
  83.2 7.3 %collective-permute-start.9 = (f32[1,40,256]{2,1,0:T(8,128)S(1)}, f32[1,40,256]{2,1,0:T(8,128)S(1)}, u32[]{:S(2)}, u32[]{:S(2)}) collective-permute-start(f32[1,40,256]{2,1,0:T(8,128)S(1)} %get-tuple-element.18), channel_id=1, source_target_pairs={{0,20},{4,24},{8,28},{12,0},{16,4},{20,8},{24,12},{28,16},{1,21},{... | collective-permute-start | bytes 122888 | tf_op jit(solution)/shard_map/ppermute | solution.py:16
  87.1 4.4 %collective-permute-start.10 = (f32[1,40,256]{2,1,0:T(8,128)S(1)}, f32[1,40,256]{2,1,0:T(8,128)S(1)}, u32[]{:S(2)}, u32[]{:S(2)}) collective-permute-start(f32[1,40,256]{2,1,0:T(8,128)S(1)} %get-tuple-element.17), channel_id=1, source_target_pairs={{0,16},{4,20},{8,24},{12,28},{16,0},{20,4},{24,8},{28,12},{1,17},{... | collective-permute-start | bytes 122888 | tf_op jit(solution)/shard_map/ppermute | solution.py:16
  87.3 4.2 %collective-permute-start.11 = (f32[1,40,256]{2,1,0:T(8,128)S(1)}, f32[1,40,256]{2,1,0:T(8,128)S(1)}, u32[]{:S(2)}, u32[]{:S(2)}) collective-permute-start(f32[1,40,256]{2,1,0:T(8,128)S(1)} %get-tuple-element.16), channel_id=1, source_target_pairs={{0,12},{4,16},{8,20},{12,24},{16,28},{20,0},{24,4},{28,8},{1,13},{... | collective-permute-start | bytes 122888 | tf_op jit(solution)/shard_map/ppermute | solution.py:16
  88.8 4.9 %collective-permute-start.12 = (f32[1,40,256]{2,1,0:T(8,128)S(1)}, f32[1,40,256]{2,1,0:T(8,128)S(1)}, u32[]{:S(2)}, u32[]{:S(2)}) collective-permute-start(f32[1,40,256]{2,1,0:T(8,128)S(1)} %get-tuple-element.15), channel_id=1, source_target_pairs={{0,8},{4,12},{8,16},{12,20},{16,24},{20,28},{24,0},{28,4},{1,9},{5... | collective-permute-start | bytes 122888 | tf_op jit(solution)/shard_map/ppermute | solution.py:16
  90.4 4.3 %collective-permute-start.13 = (f32[1,40,256]{2,1,0:T(8,128)S(1)}, f32[1,40,256]{2,1,0:T(8,128)S(1)}, u32[]{:S(2)}, u32[]{:S(2)}) collective-permute-start(f32[1,40,256]{2,1,0:T(8,128)S(1)} %get-tuple-element.14), channel_id=1, source_target_pairs={{0,4},{4,8},{8,12},{12,16},{16,20},{20,24},{24,28},{28,0},{1,5},{5... | collective-permute-start | bytes 122888 | tf_op jit(solution)/shard_map/ppermute | solution.py:16
  91.5 4.2 %copy-start.6 = (f32[256,256]{1,0:T(8,128)S(1)}, f32[256,256]{1,0:T(8,128)}, u32[]{:S(2)}) copy-start(f32[256,256]{1,0:T(8,128)} %param.18) | copy-start | bytes 786436
  94.9 1.2 %copy-start.7 = (f32[256,256]{1,0:T(8,128)S(1)}, f32[256,256]{1,0:T(8,128)}, u32[]{:S(2)}) copy-start(f32[256,256]{1,0:T(8,128)} %param.20) | copy-start | bytes 786436
  95.6 2.2 %collective-permute-start.14 = (f32[320,256]{1,0:T(8,128)S(1)}, f32[320,256]{1,0:T(8,128)S(1)}, u32[]{:S(2)}, u32[]{:S(2)}) collective-permute-start(f32[320,256]{1,0:T(8,128)S(1)} %fusion.62), channel_id=1, source_target_pairs={{0,4},{4,0},{8,12},{12,8},{16,20},{20,16},{24,28},{28,24},{1,5},{5... | collective-permute-start | bytes 983048 | tf_op jit(solution)/shard_map/ppermute | solution.py:45
  96.6 3.3 %collective-permute-start.15 = (f32[320,256]{1,0:T(8,128)S(1)}, f32[320,256]{1,0:T(8,128)S(1)}, u32[]{:S(2)}, u32[]{:S(2)}) collective-permute-start(f32[320,256]{1,0:T(8,128)S(1)} %fusion.63), channel_id=1, source_target_pairs={{0,4},{4,0},{8,12},{12,8},{16,20},{20,16},{24,28},{28,24},{1,5},{5... | collective-permute-start | bytes 983048 | tf_op jit(solution)/shard_map/ppermute | solution.py:45
  98.7 2.2 %copy-start.8 = (f32[256,256]{1,0:T(8,128)S(1)}, f32[256,256]{1,0:T(8,128)}, u32[]{:S(2)}) copy-start(f32[256,256]{1,0:T(8,128)} %param.21) | copy-start | bytes 786436
